TPU v7x, 32 devices: a whole 2x2x4 slice. The times are simulated.
32 devices in a mesh: cell: 8 (over z, y), grp: 4 (over x, core).
Axes of the slice: x: 2, y: 2, z: 4, core: 2. Of those that a mesh axis runs over, the one named last changes fastest.
Arguments:
- initial_guess: float32 [9, 6144], P(None, 'cell'), may hold values from -3 to 3
- right_side: float32 [9, 6144], P(None, 'cell')
- camera_blocks: float32 [9, 9, 6144], P(None, None, 'cell'), as said below
- point_inverse: float32 [3, 3, 16384], P(None, None, ('cell', 'grp')), as said below
- jacobian_tiles: bfloat16 [192, 576, 384], P(('cell', 'grp'))
- tile_pattern: int32 [192, 2], P(('cell', 'grp')), may hold values from 0 to 35, as said below
- cell_load: int32 [8], P('cell'), may hold values from 2 to 6, as said below
Outputs:
- solution: float32 [9, 6144], P(None, 'cell')
- residual: float32 [9, 6144], P(None, 'cell')
Inputs may be any that keep to these rules, and one draw needn't show every extreme that they name: `tile_pattern`: column 0 is below 36, column 1 below 4. `cell_load`: A quarter of the cells, rounded down, chosen from the seed, have 6 live slots on each of their devices; every other cell has 2. Slots at or past the load are unused. `camera_blocks`: each camera block is symmetric with a dominant diagonal. `point_inverse`: each point's block is symmetric with a dominant diagonal.
All inputs are finite; a program needn't handle non-finite values.
Results may differ from a plain program's by a relative error of at most 0.0095.
Values may be sent and summed in bfloat16 or wider, within the bound.
A program may use at most 64 MiB of HBM per device.

v0:
```python
import jax
import jax.numpy as jnp
from jax import lax
from jax.sharding import PartitionSpec as P

CAM_PARAMS = 9
PT_PARAMS = 3
CAM_TILE = 64
PT_TILE = 128
CAM_TILES = 12
PT_TILES = 4
SLOTS = 6
ITERS = 2


HIGHEST = lax.Precision.HIGHEST


def extended(array, sides, width):
    for axis, dim in sides:
        size, length = (lax.axis_size(axis), array.shape[dim])
        up = [(i, (i + 1) % size) for i in range(size)]
        down = [(j, i) for i, j in up]
        last = lax.slice_in_dim(array, length - width, length, axis=dim)
        first = lax.slice_in_dim(array, 0, width, axis=dim)
        before = lax.ppermute(last, axis, up)
        after = lax.ppermute(first, axis, down)
        array = jnp.concatenate([before, array, after], axis=dim)
    return array


def shifted(array, axis, by):
    length = lax.axis_size(axis)
    return lax.ppermute(array, axis, [(i, (i + by) % length) for i in range(length)])


def tile_rows(camera_field, tile_width):
    components = camera_field.shape[0]
    return (
        camera_field.reshape(components, -1, tile_width)
        .transpose(1, 0, 2)
        .reshape(-1, components * tile_width)
    )


def field_columns(row_block, components):
    tile_width = row_block.shape[1] // components
    return row_block.reshape(-1, components, tile_width).transpose(1, 0, 2).reshape(components, -1)


def per_device(
    initial_guess, right_side, camera_blocks, point_inverse, jacobian_tiles, tile_pattern, cell_load
):
    camera_count = initial_guess.shape[1]
    window_ids = tile_pattern[:, 0]
    point_ids = tile_pattern[:, 1]
    live_mask = (lax.iota(jnp.int32, SLOTS) < cell_load[0]).astype(jnp.float32)
    pick_window = window_ids[:, None] == lax.iota(jnp.int32, 3 * CAM_TILES)[None, :]
    pick_point = point_ids[:, None] == lax.iota(jnp.int32, PT_TILES)[None, :]
    diagonal_part = jnp.diagonal(camera_blocks, axis1=0, axis2=1).T
    inverse = point_inverse.reshape(PT_PARAMS, PT_PARAMS, PT_TILES, PT_TILE)
    point_width = PT_PARAMS * PT_TILE

    def apply_schur(direction):
        lowered = direction.astype(jnp.bfloat16)
        window = extended(lowered, (("cell", 1),), camera_count)
        window_rows = tile_rows(window, CAM_TILE)
        chosen = jnp.dot(
            pick_window.astype(jnp.bfloat16), window_rows, preferred_element_type=jnp.float32
        ).astype(jnp.bfloat16)
        forward = (
            jnp.einsum("tk,tkj->tj", chosen, jacobian_tiles, preferred_element_type=jnp.float32)
            * live_mask[:, None]
        )
        point_sums = jnp.dot(pick_point.astype(jnp.float32).T, forward, precision=HIGHEST)
        sectioned = point_sums.reshape(PT_TILES, PT_PARAMS, PT_TILE)
        solved = (
            jnp.einsum("jipq,piq->pjq", inverse, sectioned, precision=HIGHEST)
            .reshape(PT_TILES, point_width)
            .astype(jnp.bfloat16)
        )
        gathered = jnp.dot(
            pick_point.astype(jnp.bfloat16), solved, preferred_element_type=jnp.float32
        ).astype(jnp.bfloat16)
        backward = (
            jnp.einsum("tj,tkj->tk", gathered, jacobian_tiles, preferred_element_type=jnp.float32)
            * live_mask[:, None]
        )
        window_sums = jnp.dot(pick_window.astype(jnp.float32).T, backward, precision=HIGHEST)
        partial_field = field_columns(window_sums, CAM_PARAMS)
        summed = lax.psum(partial_field.astype(jnp.bfloat16), "grp").astype(jnp.float32)
        from_left = shifted(summed[:, 2 * camera_count :], "cell", 1)
        from_right = shifted(summed[:, :camera_count], "cell", -1)
        back_total = summed[:, camera_count : 2 * camera_count] + from_left + from_right
        return jnp.einsum("klc,lc->kc", camera_blocks, direction, precision=HIGHEST) - back_total

    solution = initial_guess
    residual = right_side - apply_schur(solution)
    precond = residual / diagonal_part
    direction = precond
    rz_now = lax.psum(jnp.sum(residual * precond), "cell")
    for iteration in range(ITERS):
        image = apply_schur(direction)
        scaled_image = image / diagonal_part
        curvature_value, cross_term, square = lax.psum(
            (jnp.sum(direction * image), jnp.sum(image * precond), jnp.sum(image * scaled_image)),
            "cell",
        )
        step_size = rz_now / curvature_value
        solution = solution + step_size * direction
        residual = residual - step_size * image
        precond = residual / diagonal_part
        rz_next = rz_now - 2.0 * step_size * cross_term + step_size * step_size * square
        direction = precond + rz_next / rz_now * direction
        rz_now = rz_next
    return (solution, residual)


def solution(mesh):
    placed = (
        P(None, "cell"),
        P(None, "cell"),
        P(None, None, "cell"),
        P(None, None, ("cell", "grp")),
        P(("cell", "grp"), None, None),
        P(("cell", "grp"), None),
        P("cell"),
    )
    return jax.shard_map(
        per_device,
        mesh=mesh,
        in_specs=placed,
        out_specs=(P(None, "cell"), P(None, "cell")),
        check_vma=False,
    )
```

profile of v0, /device:TPU:0, one launch (start us, length us, event | category | flops | bytes accessed | tf_op | source)
XLA Modules:
  0.0 142.2 jit_solution(16594648652979509193)
XLA Ops:
  0.6 1.0 convert_element_type.118
  1.6 6.0 %collective-permute-start.1 = (bf16[9,768]{1,0:T(8,128)(2,1)S(1)}, bf16[9,768]{1,0:T(8,128)(2,1)S(1)}, u32[]{:S(2)}, u32[]{:S(2)}) collective-permute-start(bf16[9,768]{1,0:T(8,128)(2,1)S(1)} %convert_element_type.118), channel_id=1, source_target_pairs={{4,0},{8,4},{12,8},{16,12},{20,16},{24,20},{28,24},{0,28},{5,1},{9... | collective-permute-start | bytes 41480 | tf_op jit(solution)/shard_map/ppermute | solution.py:27
  7.6 0.8 slice_bitcast_fusion
  9.0 1.1 multiply_reduce_fusion.2
  10.2 0.8 reshape.60
  10.9 3.2 %collective-permute-done = bf16[9,768]{1,0:T(8,128)(2,1)S(1)} collective-permute-done((bf16[9,768]{1,0:T(8,128)(2,1)S(1)}, bf16[9,768]{1,0:T(8,128)(2,1)S(1)}, u32[]{:S(2)}, u32[]{:S(2)}) %collective-permute-start) | collective-permute-done | bytes 13856 | tf_op jit(solution)/shard_map/ppermute | solution.py:26
  14.7 0.5 fusion.21
  15.6 0.8 fusion.33
  16.4 0.3 convolution_convert_fusion.2
  17.1 10.9 %psum.52 = bf16[9,2304]{1,0:T(8,128)(2,1)S(1)} all-reduce(bf16[9,2304]{1,0:T(8,128)(2,1)S(1)} %convert_element_type.128), channel_id=1, replica_groups=mesh['cell'=8,'grp'=4] {'grp'}, use_global_device_ids=true, to_apply=%region_0.1 | all-reduce | flops 20736 | bytes 82944 | tf_op jit(solution)/shard_map/psum | solution.py:91
  28.0 0.6 fusion.63
  28.7 1.9 %collective-permute-start.3 = (f32[9,768]{1,0:T(8,128)}, f32[9,768]{1,0:T(8,128)S(1)}, u32[]{:S(2)}, u32[]{:S(2)}) collective-permute-start(f32[9,768]{1,0:T(8,128)} %get-tuple-element.21), channel_id=1, source_target_pairs={{0,28},{4,0},{8,4},{12,8},{16,12},{20,16},{24,20},{28,24},{1,29},{... | collective-permute-start | bytes 82952 | tf_op jit(solution)/shard_map/ppermute | solution.py:34
  30.7 0.7 gather_fusion
  31.4 1.6 %collective-permute-done.3 = f32[9,768]{1,0:T(8,128)S(1)} collective-permute-done((f32[9,768]{1,0:T(8,128)}, f32[9,768]{1,0:T(8,128)S(1)}, u32[]{:S(2)}, u32[]{:S(2)}) %collective-permute-start.3) | collective-permute-done | bytes 27680 | tf_op jit(solution)/shard_map/ppermute | solution.py:34
  33.0 0.6 copy-done.3
  33.6 4.1 %collective-permute-done.2 = f32[9,768]{1,0:T(8,128)} collective-permute-done((f32[9,768]{1,0:T(8,128)}, f32[9,768]{1,0:T(8,128)}, u32[]{:S(2)}, u32[]{:S(2)}) %collective-permute-start.2) | collective-permute-done | bytes 27680 | tf_op jit(solution)/shard_map/ppermute | solution.py:34
  37.7 0.9 fusion.59
  38.5 0.6 collective-permute-start.5
  39.1 1.5 %collective-permute-start.4 = (bf16[9,768]{1,0:T(8,128)(2,1)S(1)}, bf16[9,768]{1,0:T(8,128)(2,1)S(1)}, u32[]{:S(2)}, u32[]{:S(2)}) collective-permute-start(bf16[9,768]{1,0:T(8,128)(2,1)S(1)} %get-tuple-element.13), channel_id=1, source_target_pairs={{0,4},{4,8},{8,12},{12,16},{16,20},{20,24},{24,28},{28,0},{1,5},{5... | collective-permute-start | bytes 41480 | tf_op jit(solution)/shard_map/ppermute | solution.py:26
  40.6 1.8 %collective-permute-done.5 = bf16[9,768]{1,0:T(8,128)(2,1)S(1)} collective-permute-done((bf16[9,768]{1,0:T(8,128)(2,1)S(1)}, bf16[9,768]{1,0:T(8,128)(2,1)S(1)}, u32[]{:S(2)}, u32[]{:S(2)}) %collective-permute-start.5) | collective-permute-done | bytes 13856 | tf_op jit(solution)/shard_map/ppermute | solution.py:27
  42.4 3.2 %collective-permute-done.4 = bf16[9,768]{1,0:T(8,128)(2,1)S(1)} collective-permute-done((bf16[9,768]{1,0:T(8,128)(2,1)S(1)}, bf16[9,768]{1,0:T(8,128)(2,1)S(1)}, u32[]{:S(2)}, u32[]{:S(2)}) %collective-permute-start.4) | collective-permute-done | bytes 13856 | tf_op jit(solution)/shard_map/ppermute | solution.py:26
  46.1 0.5 fusion.19
  47.1 0.8 fusion.31
  48.5 10.9 %psum.54 = bf16[9,2304]{1,0:T(8,128)(2,1)S(1)} all-reduce(bf16[9,2304]{1,0:T(8,128)(2,1)S(1)} %convert_element_type.139), channel_id=1, replica_groups=mesh['cell'=8,'grp'=4] {'grp'}, use_global_device_ids=true, to_apply=%region_3.4 | all-reduce | flops 20736 | bytes 82944 | tf_op jit(solution)/shard_map/psum | solution.py:91
  59.6 2.0 %collective-permute-start.6 = (f32[9,768]{1,0:T(8,128)S(1)}, f32[9,768]{1,0:T(8,128)S(1)}, u32[]{:S(2)}, u32[]{:S(2)}) collective-permute-start(f32[9,768]{1,0:T(8,128)S(1)} %get-tuple-element.18), channel_id=1, source_target_pairs={{0,4},{4,8},{8,12},{12,16},{16,20},{20,24},{24,28},{28,0},{1,5},{5... | collective-permute-start | bytes 82952 | tf_op jit(solution)/shard_map/ppermute | solution.py:34
  61.7 2.0 %collective-permute-done.7 = f32[9,768]{1,0:T(8,128)S(1)} collective-permute-done((f32[9,768]{1,0:T(8,128)S(1)}, f32[9,768]{1,0:T(8,128)S(1)}, u32[]{:S(2)}, u32[]{:S(2)}) %collective-permute-start.7) | collective-permute-done | bytes 27680 | tf_op jit(solution)/shard_map/ppermute | solution.py:34
  63.6 2.8 %collective-permute-done.6 = f32[9,768]{1,0:T(8,128)S(1)} collective-permute-done((f32[9,768]{1,0:T(8,128)S(1)}, f32[9,768]{1,0:T(8,128)S(1)}, u32[]{:S(2)}, u32[]{:S(2)}) %collective-permute-start.6) | collective-permute-done | bytes 27680 | tf_op jit(solution)/shard_map/ppermute | solution.py:34
  66.4 0.7 fusion.13
  67.1 17.8 %all-reduce = (f32[]{:T(128)}, f32[]{:T(128)}, f32[]{:T(128)}) all-reduce(f32[]{:T(128)} %get-tuple-element.4, f32[]{:T(128)} %get-tuple-element.3, f32[]{:T(128)} %get-tuple-element.2), channel_id=1, replica_groups=mesh['cell'=8,'grp'=4] {'cell'}, use_global_device_ids=true, to_apply=%region_2.3 | all-reduce | flops 3 | bytes 24 | tf_op jit(solution)/shard_map/psum | solution.py:101
  88.6 2.1 %collective-permute-start.9 = (bf16[9,768]{1,0:T(8,128)(2,1)S(1)}, bf16[9,768]{1,0:T(8,128)(2,1)S(1)}, u32[]{:S(2)}, u32[]{:S(2)}) collective-permute-start(bf16[9,768]{1,0:T(8,128)(2,1)S(1)} %get-tuple-element.10), channel_id=1, source_target_pairs={{4,0},{8,4},{12,8},{16,12},{20,16},{24,20},{28,24},{0,28},{5,1},{9... | collective-permute-start | bytes 41480 | tf_op jit(solution)/shard_map/ppermute | solution.py:27
  90.7 1.8 %collective-permute-done.9 = bf16[9,768]{1,0:T(8,128)(2,1)S(1)} collective-permute-done((bf16[9,768]{1,0:T(8,128)(2,1)S(1)}, bf16[9,768]{1,0:T(8,128)(2,1)S(1)}, u32[]{:S(2)}, u32[]{:S(2)}) %collective-permute-start.9) | collective-permute-done | bytes 13856 | tf_op jit(solution)/shard_map/ppermute | solution.py:27
  92.5 4.7 %collective-permute-done.8 = bf16[9,768]{1,0:T(8,128)(2,1)S(1)} collective-permute-done((bf16[9,768]{1,0:T(8,128)(2,1)S(1)}, bf16[9,768]{1,0:T(8,128)(2,1)S(1)}, u32[]{:S(2)}, u32[]{:S(2)}) %collective-permute-start.8) | collective-permute-done | bytes 13856 | tf_op jit(solution)/shard_map/ppermute | solution.py:26
  97.2 0.7 reshape.64
  97.9 0.9 copy.114
  98.9 0.8 reshape.65
  99.6 1.0 fusion.2
  100.6 0.5 fusion.17
  101.6 0.8 fusion.29
  102.4 0.3 convolution_convert_fusion
  102.9 0.6 copy.17
  103.5 1.0 convert_element_type.150
  104.5 10.9 %psum.57 = bf16[9,2304]{1,0:T(8,128)(2,1)S(1)} all-reduce(bf16[9,2304]{1,0:T(8,128)(2,1)S(1)} %convert_element_type.150), channel_id=1, replica_groups=mesh['cell'=8,'grp'=4] {'grp'}, use_global_device_ids=true, to_apply=%region_8.9 | all-reduce | flops 20736 | bytes 82944 | tf_op jit(solution)/shard_map/psum | solution.py:91
  115.6 2.0 %collective-permute-start.10 = (f32[9,768]{1,0:T(8,128)S(1)}, f32[9,768]{1,0:T(8,128)S(1)}, u32[]{:S(2)}, u32[]{:S(2)}) collective-permute-start(f32[9,768]{1,0:T(8,128)S(1)} %get-tuple-element.16), channel_id=1, source_target_pairs={{0,4},{4,8},{8,12},{12,16},{16,20},{20,24},{24,28},{28,0},{1,5},{5... | collective-permute-start | bytes 82952 | tf_op jit(solution)/shard_map/ppermute | solution.py:34
  117.7 2.0 %collective-permute-done.11 = f32[9,768]{1,0:T(8,128)S(1)} collective-permute-done((f32[9,768]{1,0:T(8,128)S(1)}, f32[9,768]{1,0:T(8,128)S(1)}, u32[]{:S(2)}, u32[]{:S(2)}) %collective-permute-start.11) | collective-permute-done | bytes 27680 | tf_op jit(solution)/shard_map/ppermute | solution.py:34
  119.6 2.8 %collective-permute-done.10 = f32[9,768]{1,0:T(8,128)S(1)} collective-permute-done((f32[9,768]{1,0:T(8,128)S(1)}, f32[9,768]{1,0:T(8,128)S(1)}, u32[]{:S(2)}, u32[]{:S(2)}) %collective-permute-start.10) | collective-permute-done | bytes 27680 | tf_op jit(solution)/shard_map/ppermute | solution.py:34
  122.4 0.6 multiply_reduce_fusion.3
  123.0 17.8 %psum.58 = f32[]{:T(128)} all-reduce(f32[]{:T(128)} %get-tuple-element.8), channel_id=1, replica_groups=mesh['cell'=8,'grp'=4] {'cell'}, use_global_device_ids=true, to_apply=%region_10.11 | all-reduce | flops 1 | bytes 8 | tf_op jit(solution)/shard_map/psum | solution.py:105
  141.5 0.7 multiply_subtract_fusion
  (51 shorter events, 4.0 us)
Async XLA Ops:
  0.6 14.0 %copy-start = (bf16[6,576,384]{2,1,0:T(8,128)(2,1)S(1)}, bf16[6,576,384]{2,1,0:T(8,128)(2,1)}, u32[]{:S(2)}) copy-start(bf16[6,576,384]{2,1,0:T(8,128)(2,1)} %param.11) | copy-start | bytes 7962628
  1.6 9.3 %collective-permute-start.1 = (bf16[9,768]{1,0:T(8,128)(2,1)S(1)}, bf16[9,768]{1,0:T(8,128)(2,1)S(1)}, u32[]{:S(2)}, u32[]{:S(2)}) collective-permute-start(bf16[9,768]{1,0:T(8,128)(2,1)S(1)} %convert_element_type.118), channel_id=1, source_target_pairs={{4,0},{8,4},{12,8},{16,12},{20,16},{24,20},{28,24},{0,28},{5,1},{9... | collective-permute-start | bytes 41480 | tf_op jit(solution)/shard_map/ppermute | solution.py:27
  7.6 6.5 %collective-permute-start = (bf16[9,768]{1,0:T(8,128)(2,1)S(1)}, bf16[9,768]{1,0:T(8,128)(2,1)S(1)}, u32[]{:S(2)}, u32[]{:S(2)}) collective-permute-start(bf16[9,768]{1,0:T(8,128)(2,1)S(1)} %convert_element_type.118), channel_id=1, source_target_pairs={{0,4},{4,8},{8,12},{12,16},{16,20},{20,24},{24,28},{28,0},{1,5},{5... | collective-permute-start | bytes 41480 | tf_op jit(solution)/shard_map/ppermute | solution.py:26
  15.1 15.6 %copy-start.1 = (f32[9,9,768]{2,1,0:T(8,128)S(1)}, f32[9,9,768]{2,1,0:T(8,128)}, u32[]{:S(2)}) copy-start(f32[9,9,768]{2,1,0:T(8,128)} %param.9) | copy-start | bytes 746500
  28.7 4.3 %collective-permute-start.3 = (f32[9,768]{1,0:T(8,128)}, f32[9,768]{1,0:T(8,128)S(1)}, u32[]{:S(2)}, u32[]{:S(2)}) collective-permute-start(f32[9,768]{1,0:T(8,128)} %get-tuple-element.21), channel_id=1, source_target_pairs={{0,28},{4,0},{8,4},{12,8},{16,12},{20,16},{24,20},{28,24},{1,29},{... | collective-permute-start | bytes 82952 | tf_op jit(solution)/shard_map/ppermute | solution.py:34
  30.6 7.1 %collective-permute-start.2 = (f32[9,768]{1,0:T(8,128)}, f32[9,768]{1,0:T(8,128)}, u32[]{:S(2)}, u32[]{:S(2)}) collective-permute-start(f32[9,768]{1,0:T(8,128)} %get-tuple-element.20), channel_id=1, source_target_pairs={{0,4},{4,8},{8,12},{12,16},{16,20},{20,24},{24,28},{28,0},{1,5},{5... | collective-permute-start | bytes 82952 | tf_op jit(solution)/shard_map/ppermute | solution.py:34
  33.0 0.6 copy-start.3
  38.5 3.9 %collective-permute-start.5 = (bf16[9,768]{1,0:T(8,128)(2,1)S(1)}, bf16[9,768]{1,0:T(8,128)(2,1)S(1)}, u32[]{:S(2)}, u32[]{:S(2)}) collective-permute-start(bf16[9,768]{1,0:T(8,128)(2,1)S(1)} %get-tuple-element.13), channel_id=1, source_target_pairs={{4,0},{8,4},{12,8},{16,12},{20,16},{24,20},{28,24},{0,28},{5,1},{9... | collective-permute-start | bytes 41480 | tf_op jit(solution)/shard_map/ppermute | solution.py:27
  39.1 6.5 %collective-permute-start.4 = (bf16[9,768]{1,0:T(8,128)(2,1)S(1)}, bf16[9,768]{1,0:T(8,128)(2,1)S(1)}, u32[]{:S(2)}, u32[]{:S(2)}) collective-permute-start(bf16[9,768]{1,0:T(8,128)(2,1)S(1)} %get-tuple-element.13), channel_id=1, source_target_pairs={{0,4},{4,8},{8,12},{12,16},{16,20},{20,24},{24,28},{28,0},{1,5},{5... | collective-permute-start | bytes 41480 | tf_op jit(solution)/shard_map/ppermute | solution.py:26
  59.5 4.1 %collective-permute-start.7 = (f32[9,768]{1,0:T(8,128)S(1)}, f32[9,768]{1,0:T(8,128)S(1)}, u32[]{:S(2)}, u32[]{:S(2)}) collective-permute-start(f32[9,768]{1,0:T(8,128)S(1)} %get-tuple-element.19), channel_id=1, source_target_pairs={{0,28},{4,0},{8,4},{12,8},{16,12},{20,16},{24,20},{28,24},{1,29},{... | collective-permute-start | bytes 82952 | tf_op jit(solution)/shard_map/ppermute | solution.py:34
  59.6 6.8 %collective-permute-start.6 = (f32[9,768]{1,0:T(8,128)S(1)}, f32[9,768]{1,0:T(8,128)S(1)}, u32[]{:S(2)}, u32[]{:S(2)}) collective-permute-start(f32[9,768]{1,0:T(8,128)S(1)} %get-tuple-element.18), channel_id=1, source_target_pairs={{0,4},{4,8},{8,12},{12,16},{16,20},{20,24},{24,28},{28,0},{1,5},{5... | collective-permute-start | bytes 82952 | tf_op jit(solution)/shard_map/ppermute | solution.py:34
  88.6 3.9 %collective-permute-start.9 = (bf16[9,768]{1,0:T(8,128)(2,1)S(1)}, bf16[9,768]{1,0:T(8,128)(2,1)S(1)}, u32[]{:S(2)}, u32[]{:S(2)}) collective-permute-start(bf16[9,768]{1,0:T(8,128)(2,1)S(1)} %get-tuple-element.10), channel_id=1, source_target_pairs={{4,0},{8,4},{12,8},{16,12},{20,16},{24,20},{28,24},{0,28},{5,1},{9... | collective-permute-start | bytes 41480 | tf_op jit(solution)/shard_map/ppermute | solution.py:27
  90.7 6.5 %collective-permute-start.8 = (bf16[9,768]{1,0:T(8,128)(2,1)S(1)}, bf16[9,768]{1,0:T(8,128)(2,1)S(1)}, u32[]{:S(2)}, u32[]{:S(2)}) collective-permute-start(bf16[9,768]{1,0:T(8,128)(2,1)S(1)} %get-tuple-element.10), channel_id=1, source_target_pairs={{0,4},{4,8},{8,12},{12,16},{16,20},{20,24},{24,28},{28,0},{1,5},{5... | collective-permute-start | bytes 41480 | tf_op jit(solution)/shard_map/ppermute | solution.py:26
  101.1 40.4 %copy-start.2 = (f32[9,768]{1,0:T(8,128)S(1)}, f32[9,768]{1,0:T(8,128)}, u32[]{:S(2)}) copy-start(f32[9,768]{1,0:T(8,128)} %param.7) | copy-start | bytes 82948
  115.5 4.1 %collective-permute-start.11 = (f32[9,768]{1,0:T(8,128)S(1)}, f32[9,768]{1,0:T(8,128)S(1)}, u32[]{:S(2)}, u32[]{:S(2)}) collective-permute-start(f32[9,768]{1,0:T(8,128)S(1)} %get-tuple-element.17), channel_id=1, source_target_pairs={{0,28},{4,0},{8,4},{12,8},{16,12},{20,16},{24,20},{28,24},{1,29},{... | collective-permute-start | bytes 82952 | tf_op jit(solution)/shard_map/ppermute | solution.py:34
  115.6 6.8 %collective-permute-start.10 = (f32[9,768]{1,0:T(8,128)S(1)}, f32[9,768]{1,0:T(8,128)S(1)}, u32[]{:S(2)}, u32[]{:S(2)}) collective-permute-start(f32[9,768]{1,0:T(8,128)S(1)} %get-tuple-element.16), channel_id=1, source_target_pairs={{0,4},{4,8},{8,12},{12,16},{16,20},{20,24},{24,28},{28,0},{1,5},{5... | collective-permute-start | bytes 82952 | tf_op jit(solution)/shard_map/ppermute | solution.py:34
where the time goes:
time: 143 us; the launch traced here: 142 us
  blocking collectives  68.4 us (48%)
  waiting for transfers between devices  29.8 us (21%)
  starting transfers between devices  16.4 us (11%)
  local copies, waits for them, and re-layouts  8.84 us (6%)
  matrix products  7.59 us (5%)
  between operations  5.93 us (4%)
  other arithmetic  5.24 us (4%)
    psum x3, blocking collectives, apply_schur(): lax.psum(partial_field.astype(jnp.bfloat16), 'grp').astype(jnp.float32)  32.8 us
    psum x1, blocking collectives, per_device(): lax.psum((jnp.sum(direction * image), jnp.sum(image * precond), jnp.sum(i...  17.8 us
    psum x1, blocking collectives, per_device(): rz_now = lax.psum(jnp.sum(residual * precond), 'cell')  17.8 us
    ppermute x6, waiting for transfers between devices, shifted(): lax.ppermute(array, axis, [(i, (i + by) % length) for i in range(length)])  15.1 us
    ppermute x3, waiting for transfers between devices, extended(): before = lax.ppermute(last, axis, up)  11.1 us
    ppermute x3, starting transfers between devices, extended(): after = lax.ppermute(first, axis, down)  8.66 us
    ppermute x6, starting transfers between devices, shifted(): lax.ppermute(array, axis, [(i, (i + by) % length) for i in range(length)])  6.17 us
    ppermute x3, waiting for transfers between devices, extended(): after = lax.ppermute(first, axis, down)  3.56 us
  transfers between devices with their start and end apart: 12, of which 11 were waited for; matrix products, arithmetic and copies ran while one was open for 2% of the time, Pallas kernels for 0%

commit v1 on v0

v1 whole, which is shorter than its diff:
```python
import functools

import jax
import jax.numpy as jnp
from jax import lax
from jax.experimental import pallas as pl
from jax.experimental.pallas import tpu as pltpu
from jax.sharding import PartitionSpec as P

CAM_TILE = 64
ITERS = 2
REACH = 2
SPAN = 2 * REACH + 1
LANES = 128
ROWS = 8
MESH = pl.DeviceIdType.MESH
F32 = jnp.float32
BF16 = jnp.bfloat16


def kernel(
    cells,
    grps,
    guess_hbm,
    right_hbm,
    blocks_hbm,
    inverse_hbm,
    jac_hbm,
    pattern,
    load,
    solution_ref,
    residual_ref,
    guess,
    right,
    blocks,
    inverse,
    jac,
    window,
    guess_send,
    guess_recv,
    halo_send,
    halo_recv,
    image_send,
    image_recv,
    pattern_send,
    pattern_recv,
    slot_send,
    slot_recv,
    scalar_send,
    scalar_recv,
    local_sem,
    jac_sem,
    halo_send_sem,
    halo_recv_sem,
    image_send_sem,
    image_recv_sem,
    pattern_sem,
    slot_send_sem,
    slot_recv_sem,
    scalar_sem,
):
    params, cameras = guess.shape
    slots, rows_wide, points_wide = jac.shape
    tiles = cameras // CAM_TILE
    pairs = cameras // LANES
    coords = inverse.shape[0]
    point_tiles = inverse.shape[2] // LANES
    devices = cells * grps
    cell = lax.axis_index("cell")
    grp = lax.axis_index("grp")
    me = cell * grps + grp

    local = [
        pltpu.make_async_copy(src, dst, local_sem.at[i])
        for i, (src, dst) in enumerate(
            ((guess_hbm, guess), (blocks_hbm, blocks), (right_hbm, right), (inverse_hbm, inverse))
        )
    ]
    jac_copies = [
        pltpu.make_async_copy(jac_hbm.at[s], jac.at[s], jac_sem.at[s]) for s in range(slots)
    ]
    for copy in local:
        copy.start()
    for copy in jac_copies:
        copy.start()

    barrier = pltpu.get_barrier_semaphore()

    def greet(i, carry):
        other = lax.rem(me + i, devices)
        pl.semaphore_signal(
            barrier, inc=1, device_id=(other // grps, lax.rem(other, grps)), device_id_type=MESH
        )
        return carry

    lax.fori_loop(1, devices, greet, 0)

    def near(delta, turn):
        return (lax.rem(cell + delta + cells, cells), lax.rem(grp + turn, grps))

    def slot_index(delta, turn):
        return (delta % SPAN) * grps + turn % grps

    def peers(reach):
        found = []
        for delta in sorted(range(-reach, reach + 1), key=lambda d: -abs(d)):
            for turn in range(grps):
                if delta != 0 or turn != 0:
                    found.append((delta, turn))
        return found

    def iota(shape, axis):
        return lax.broadcasted_iota(jnp.int32, shape, axis)

    lane8 = iota((ROWS, LANES), 1)
    row8 = iota((ROWS, LANES), 0)
    lane9 = iota((params, LANES), 1)
    row9 = iota((params, LANES), 0)
    low9 = lane9 < CAM_TILE
    chunks = (rows_wide + LANES - 1) // LANES
    own_rows = [row9 == 2 * b + (lane9 >= CAM_TILE).astype(jnp.int32) for b in range(chunks)]

    live = [s < load[0] for s in range(slots)]
    ids = [pattern[s, 0] for s in range(slots)]
    point_ids = [pattern[s, 1] for s in range(slots)]
    id_rows = jnp.full((ROWS, LANES), -4096, jnp.int32)
    point_rows = jnp.full((ROWS, LANES), -1, jnp.int32)
    for s in range(slots):
        id_rows = jnp.where(row8 == s, jnp.where(live[s], ids[s], -4096), id_rows)
        point_rows = jnp.where(row8 == s, point_ids[s], point_rows)
    pattern_send[...] = id_rows
    pattern_recv[0] = id_rows

    def pack(field):
        tail = jnp.zeros((ROWS, LANES), F32)
        for i in range(pairs):
            tail = jnp.where(row8 == i, field[ROWS:, i * LANES : (i + 1) * LANES], tail)
        return jnp.concatenate([field[:ROWS], tail], axis=1)

    def unpack(packed):
        return [
            jnp.concatenate(
                [packed[:, i * LANES : (i + 1) * LANES], packed[i : i + 1, cameras:]], axis=0
            )
            for i in range(pairs)
        ]

    def blocks_of(field):
        return [field[:, i * LANES : (i + 1) * LANES] for i in range(pairs)]

    local[0].wait()
    guess_send[...] = pack(guess[...]).astype(BF16)
    local[1].wait()

    def block_product(field):
        total = blocks[0] * field[0:1, :]
        for k in range(1, params):
            total = total + blocks[k] * field[k : k + 1, :]
        return total

    row_wide = iota((params, cameras), 0)
    diagonal = blocks[0]
    for k in range(1, params):
        diagonal = jnp.where(row_wide == k, blocks[k], diagonal)
    scale = 1.0 / diagonal
    local[2].wait()
    residual0 = right[...] - block_product(guess[...])
    halo_send[0] = pack(residual0 * scale)
    halo_send[1] = pack(scale)
    local[3].wait()
    inverse_rows = []
    for j in range(coords):
        for i in range(coords):
            picked = jnp.zeros((ROWS, LANES), F32)
            for q in range(point_tiles):
                picked = jnp.where(
                    point_rows == q, inverse[j, i : i + 1, q * LANES : (q + 1) * LANES], picked
                )
            inverse_rows.append(picked)
    pad = jnp.zeros((ROWS, chunks * LANES - rows_wide), F32)

    pl.semaphore_wait(barrier, devices - 1)

    halo_copies = []
    for part in range(3):
        for side, delta in ((0, 1), (1, -1)):
            copy = pltpu.make_async_remote_copy(
                src_ref=guess_send if part == 0 else halo_send.at[part - 1],
                dst_ref=guess_recv.at[side] if part == 0 else halo_recv.at[side, part - 1],
                send_sem=halo_send_sem.at[side, part],
                recv_sem=halo_recv_sem.at[side, part],
                device_id=near(delta, 0),
                device_id_type=MESH,
            )
            halo_copies.append(copy)
    halo_copies[0].start()
    halo_copies[1].start()
    for delta, turn in peers(REACH):
        pltpu.make_async_remote_copy(
            src_ref=pattern_send,
            dst_ref=pattern_recv.at[slot_index(-delta, -turn)],
            send_sem=pattern_sem.at[0],
            recv_sem=pattern_sem.at[1],
            device_id=near(delta, turn),
            device_id_type=MESH,
        ).start()
    for copy in halo_copies[2:]:
        copy.start()

    def put(side, parts):
        for i in range(pairs):
            window[side * pairs + i] = parts[i]

    def slot_rows():
        forward = jnp.zeros((ROWS, points_wide), F32)
        row_points = iota((ROWS, points_wide), 0)
        for s in range(slots):
            block = window[lax.shift_right_logical(ids[s], 1)]
            turned = pltpu.roll(block, CAM_TILE, 1)
            odd = lax.bitwise_and(ids[s], 1)
            keep = jnp.where(low9, 0, 1) == odd
            tile = jnp.where(keep, block, turned)
            tile = jnp.where(live[s], tile, 0.0)
            spread = jnp.concatenate([jnp.where(own, tile, 0.0) for own in own_rows], axis=1)
            left = spread[:, :rows_wide].astype(BF16)
            product = jnp.dot(left, jac[s], preferred_element_type=F32)
            total = jnp.sum(product, axis=0, keepdims=True)
            forward = jnp.where(row_points == s, total, forward)
        wide_points = jnp.concatenate([point_rows] * coords, axis=1)
        sums = jnp.zeros((ROWS, points_wide), F32)
        for s in range(slots):
            sums = sums + jnp.where(wide_points == point_ids[s], forward[s : s + 1, :], 0.0)
        solved = []
        for j in range(coords):
            total = inverse_rows[j * coords] * sums[:, :LANES]
            for i in range(1, coords):
                total = total + inverse_rows[j * coords + i] * sums[:, i * LANES : (i + 1) * LANES]
            solved.append(total)
        solved = jnp.concatenate(solved, axis=1).astype(BF16)
        energy = forward * solved.astype(F32)
        backward = jnp.zeros((ROWS, rows_wide), F32)
        row_cams = iota((ROWS, rows_wide), 0)
        for s in range(slots):
            product = lax.dot_general(
                solved, jac[s], (((1,), (1,)), ((), ())), preferred_element_type=F32
            )
            backward = jnp.where(row_cams == s, jnp.where(live[s], product, 0.0), backward)
        backward = jnp.concatenate([backward, pad], axis=1).astype(BF16)
        energy_lanes = energy[:, :LANES]
        for i in range(1, coords):
            energy_lanes = energy_lanes + energy[:, i * LANES : (i + 1) * LANES]
        return backward, jnp.sum(energy_lanes, axis=0, keepdims=True)

    def send_slots(turn_no, backward):
        slot_send[turn_no] = backward
        slot_recv[turn_no, 0] = backward
        for delta, turn in peers(REACH):
            pltpu.make_async_remote_copy(
                src_ref=slot_send.at[turn_no],
                dst_ref=slot_recv.at[turn_no, slot_index(-delta, -turn)],
                send_sem=slot_send_sem.at[turn_no],
                recv_sem=slot_recv_sem.at[turn_no],
                device_id=near(delta, turn),
                device_id_type=MESH,
            ).start()

    others = pl.ds(1, SPAN * grps - 1)

    def wait_bytes(ref, sem):
        pltpu.make_async_copy(ref, ref, sem).wait()

    def gather_back(turn_no, chooser, sides):
        wait_bytes(slot_recv.at[turn_no, others], slot_recv_sem.at[turn_no])
        stacked = slot_recv[turn_no].astype(F32).reshape(SPAN * grps * ROWS, chunks * LANES)
        summed = jnp.dot(chooser, stacked.astype(BF16), preferred_element_type=F32)
        fields = []
        for side in sides:
            parts = []
            for i in range(pairs):
                first = side * tiles + 2 * i
                both = []
                for t in (first, first + 1):
                    total = jnp.zeros((params, LANES), F32)
                    for b in range(chunks):
                        piece = summed[t : t + 1, b * LANES : (b + 1) * LANES]
                        total = jnp.where(own_rows[b], piece, total)
                    both.append(total)
                parts.append(
                    jnp.where(low9, both[0], both[1])
                    + pltpu.roll(jnp.where(low9, both[1], both[0]), CAM_TILE, 1)
                )
            fields.append(parts)
        return fields

    put(1, blocks_of(guess[...]))
    halo_copies[0].wait()
    halo_copies[1].wait()
    put(0, unpack(guess_recv[0].astype(F32)))
    put(2, unpack(guess_recv[1].astype(F32)))
    for copy in jac_copies:
        copy.wait()
    backward, _ = slot_rows()
    send_slots(0, backward)

    wait_bytes(pattern_recv.at[others], pattern_sem.at[1])
    columns = []
    for shift in range(SPAN):
        delta = shift if shift <= REACH else shift - SPAN
        for turn in range(grps):
            at = pattern_recv[shift * grps + turn] + delta * tiles
            columns.append((at == lane8).astype(F32))
    chosen = jnp.concatenate(columns, axis=0).astype(BF16)
    unit = (iota((LANES, LANES), 0) == iota((LANES, LANES), 1)).astype(F32).astype(BF16)
    chooser = lax.dot_general(
        unit, chosen, (((1,), (1,)), ((), ())), preferred_element_type=F32
    )[: 3 * tiles].astype(BF16)
    for copy in halo_copies[2:]:
        copy.wait()

    left, own, right_side = gather_back(0, chooser, (0, 1, 2))
    residual0 = residual0 + jnp.concatenate(own, axis=1)
    direction = residual0 * scale
    put(1, blocks_of(direction))
    scales = [unpack(halo_recv[side, 1]) for side in (0, 1)]
    directions = [
        [
            start + factor * back
            for start, factor, back in zip(unpack(halo_recv[side, 0]), scales[side], backs)
        ]
        for side, backs in ((0, left), (1, right_side))
    ]
    put(0, directions[0])
    put(2, directions[1])
    product1 = block_product(direction)
    image_send[...] = pack(product1 * scale)
    image_copies = []
    for side, delta in ((0, 1), (1, -1)):
        copy = pltpu.make_async_remote_copy(
            src_ref=image_send,
            dst_ref=image_recv.at[side],
            send_sem=image_send_sem.at[side],
            recv_sem=image_recv_sem.at[side],
            device_id=near(delta, 0),
            device_id_type=MESH,
        )
        copy.start()
        image_copies.append(copy)
    backward, _ = slot_rows()
    send_slots(1, backward)
    for copy in image_copies:
        copy.wait()
    left, own, right_side = gather_back(1, chooser, (0, 1, 2))
    image1 = product1 - jnp.concatenate(own, axis=1)
    trial = residual0 - image1
    shaped = trial * scale
    put(1, blocks_of(shaped))
    for side, backs in ((0, left), (1, right_side)):
        put(
            2 * side,
            [
                start - image + factor * back
                for start, image, factor, back in zip(
                    directions[side], unpack(image_recv[side]), scales[side], backs
                )
            ],
        )
    backward, energy = slot_rows()
    send_slots(2, backward)
    product2 = block_product(shaped)

    def lane_sum(field):
        total = field[:, :LANES]
        for i in range(1, pairs):
            total = total + field[:, i * LANES : (i + 1) * LANES]
        return jnp.sum(total, axis=0, keepdims=True) * (1.0 / grps)

    sums = jnp.zeros((ROWS, LANES), F32)
    for i, value in enumerate(
        (
            lane_sum(residual0 * direction),
            lane_sum(direction * image1),
            lane_sum(residual0 * shaped),
            lane_sum(trial * shaped),
            lane_sum(image1 * shaped),
            lane_sum(shaped * product2) - energy,
        )
    ):
        sums = jnp.where(row8 == i, value, sums)
    scalar_send[...] = sums

    def spread_scalars(i, carry):
        other = lax.rem(me + i, devices)
        pltpu.make_async_remote_copy(
            src_ref=scalar_send,
            dst_ref=scalar_recv.at[i - 1],
            send_sem=scalar_sem.at[0],
            recv_sem=scalar_sem.at[1],
            device_id=(other // grps, lax.rem(other, grps)),
            device_id_type=MESH,
        ).start()
        return carry

    lax.fori_loop(1, devices, spread_scalars, 0)
    (own,) = gather_back(2, chooser, (1,))
    image2 = product2 - jnp.concatenate(own, axis=1)
    wait_bytes(scalar_recv, scalar_sem.at[1])
    totals = jnp.sum(sums + jnp.sum(scalar_recv[...], axis=0), axis=1, keepdims=True)
    rz0, curve1, cross, trial_rz, mixed, curve_w = [totals[i : i + 1, :] for i in range(6)]
    step1 = rz0 / curve1
    short = 1.0 - step1
    rz1 = short * short * rz0 + 2.0 * short * step1 * cross + step1 * step1 * trial_rz
    keep = short + rz1 / rz0
    curve2 = keep * keep * curve1 + 2.0 * keep * step1 * mixed + step1 * step1 * curve_w
    step2 = rz1 / curve2
    near_part = step1 + step2 * keep
    far_part = step2 * step1
    solution_ref[...] = guess[...] + near_part * direction + far_part * shaped
    residual_ref[...] = residual0 - near_part * image1 - far_part * image2

    wait_bytes(scalar_recv, scalar_sem.at[0])
    wait_bytes(pattern_recv.at[others], pattern_sem.at[0])
    for turn_no in range(3):
        wait_bytes(slot_recv.at[turn_no, others], slot_send_sem.at[turn_no])


def per_device(
    cells, grps, initial_guess, right_side, camera_blocks, point_inverse, jacobian_tiles, tile_pattern, cell_load
):
    params, cameras = initial_guess.shape
    slots, rows_wide, points_wide = jacobian_tiles.shape
    chunks = (rows_wide + LANES - 1) // LANES
    near = SPAN * grps
    packed = cameras + LANES
    hbm = pl.BlockSpec(memory_space=pl.ANY)
    smem = pl.BlockSpec(memory_space=pltpu.SMEM)
    vmem = pl.BlockSpec(memory_space=pltpu.VMEM)
    dma = pltpu.SemaphoreType.DMA
    field = jax.ShapeDtypeStruct((params, cameras), F32)
    return pl.pallas_call(
        functools.partial(kernel, cells, grps),
        out_shape=(field, field),
        in_specs=[hbm] * 5 + [smem] * 2,
        out_specs=(vmem, vmem),
        scratch_shapes=[
            pltpu.VMEM((params, cameras), F32),
            pltpu.VMEM((params, cameras), F32),
            pltpu.VMEM(camera_blocks.shape, F32),
            pltpu.VMEM(point_inverse.shape, F32),
            pltpu.VMEM(jacobian_tiles.shape, BF16),
            pltpu.VMEM((3 * cameras // LANES, params, LANES), F32),
            pltpu.VMEM((ROWS, packed), BF16),
            pltpu.VMEM((2, ROWS, packed), BF16),
            pltpu.VMEM((2, ROWS, packed), F32),
            pltpu.VMEM((2, 2, ROWS, packed), F32),
            pltpu.VMEM((ROWS, packed), F32),
            pltpu.VMEM((2, ROWS, packed), F32),
            pltpu.VMEM((ROWS, LANES), jnp.int32),
            pltpu.VMEM((near, ROWS, LANES), jnp.int32),
            pltpu.VMEM((3, ROWS, chunks * LANES), BF16),
            pltpu.VMEM((3, near, ROWS, chunks * LANES), BF16),
            pltpu.VMEM((ROWS, LANES), F32),
            pltpu.VMEM((cells * grps - 1, ROWS, LANES), F32),
            dma((4,)),
            dma((slots,)),
            dma((2, 3)),
            dma((2, 3)),
            dma((2,)),
            dma((2,)),
            dma((2,)),
            dma((3,)),
            dma((3,)),
            dma((2,)),
        ],
        compiler_params=pltpu.CompilerParams(collective_id=0, has_side_effects=True),
    )(initial_guess, right_side, camera_blocks, point_inverse, jacobian_tiles, tile_pattern, cell_load)


def solution(mesh):
    placed = (
        P(None, "cell"),
        P(None, "cell"),
        P(None, None, "cell"),
        P(None, None, ("cell", "grp")),
        P(("cell", "grp"), None, None),
        P(("cell", "grp"), None),
        P("cell"),
    )
    return jax.shard_map(
        functools.partial(per_device, mesh.shape["cell"], mesh.shape["grp"]),
        mesh=mesh,
        in_specs=placed,
        out_specs=(P(None, "cell"), P(None, "cell")),
        check_vma=False,
    )
```

time: 143 us -> 41.9 us (0.29)
  blocking collectives: 68.4 us -> 0 us
  Pallas kernels: 0 us -> 36.1 us
  waiting for transfers between devices: 29.8 us -> 0 us
  starting transfers between devices: 16.4 us -> 0 us
  matrix products: 7.59 us -> 0 us
  other arithmetic: 5.24 us -> 0 us
  local copies, waits for them, and re-layouts: 8.84 us -> 4.19 us
  between operations: 5.93 us -> 1.29 us
    psum x5 -> x0, blocking collectives: 68.4 us -> none  [the longest x3 32.8 us: apply_schur(): lax.psum(partial_field.astype(jnp.bfloat16), 'grp').astype(jnp.float32)]
    pallas_call x0 -> x1, Pallas kernels: none -> 36.1 us  [per_device(): pl.pallas_call(functools.partial(kernel, cells, grps), out_shape=(field,...]
    ppermute x12 -> x0, waiting for transfers between devices: 29.8 us -> none  [the longest x6 15.1 us: shifted(): lax.ppermute(array, axis, [(i, (i + by) % length) for i in range(length)])]
    ppermute x12 -> x0, starting transfers between devices: 16.4 us -> none  [the longest x3 8.66 us: extended(): after = lax.ppermute(first, axis, down)]
    dot_general x18 -> x0, matrix products: 7.59 us -> none  [the longest x3 2.43 us: apply_schur(): jnp.einsum('tj,tkj->tk', gathered, jacobian_tiles, preferred_element_type...]
    reshape x10 -> x0, local copies, waits for them, and re-layouts: 3.75 us -> none  [the longest x6 1.94 us: tile_rows(): camera_field.reshape(components, -1, tile_width).transpose(1, 0, 2)]
    unnamed x8 -> x3, local copies, waits for them, and re-layouts: 0.64 us -> 4.19 us
    convert_element_type x9 -> x0, local copies, waits for them, and re-layouts: 2.35 us -> none  [apply_schur(): partial_field.astype(jnp.bfloat16)]
  transfers between devices with their start and end apart: 12 -> 0, of which waited for: 11 -> 0; matrix products, arithmetic and copies ran while one was open for 2% -> 0% of each run, Pallas kernels for 0% -> 0%
where the time goes in v1:
time: 41.9 us; the launch traced here: 41.6 us
  Pallas kernels  36.1 us (86%)
  local copies, waits for them, and re-layouts  4.19 us (10%)
  between operations  1.29 us (3%)
    pallas_call x1, Pallas kernels, per_device(): pl.pallas_call(functools.partial(kernel, cells, grps), out_shape=(field,...  36.1 us
    unnamed x3, local copies, waits for them, and re-layouts  4.19 us

profile of v1, /device:TPU:0, one launch (start us, length us, event | category | flops | bytes accessed | tf_op | source)
XLA Modules:
  0.0 41.6 jit_solution(837182448881799876)
XLA Ops:
  1.3 1.4 %copy.9.pattern = s32[6,2]{1,0:T(8,128)} copy(s32[6,2]{0,1:T(2,128)} %param.12) | data formatting | bytes 96 | tf_op args[5]
  2.6 36.1 %shard_map.86 = (f32[9,768]{1,0:T(8,128)}, f32[9,768]{1,0:T(8,128)}) custom-call(f32[9,768]{1,0:T(8,128)} %guess_hbm.1, f32[9,768]{1,0:T(8,128)} %right_hbm.1, f32[9,9,768]{2,1,0:T(8,128)} %blocks_hbm.1, f32[3,3,512]{2,1,0:T(4,128)} %inverse_hbm.1, bf16[6,576,384]{2,1,0:T(8,128)(2,1)} %jac_hbm.1, s32[6,2]{1,0:T(8,128)} %copy.9.pattern, s32[1]{0:T(128)S(6)} %copy.12.load), custom_call_target="tpu_custom_call" | custom-call | tf_op jit(solution)/shard_map/pallas_call | solution.py:439
  38.8 1.4 %copy.13 = f32[9,768]{1,0:T(8,128)} copy(f32[9,768]{1,0:T(8,128)} %get-tuple-element.4) | data formatting | bytes 55296
  40.2 1.4 %copy.14 = f32[9,768]{1,0:T(8,128)} copy(f32[9,768]{1,0:T(8,128)} %get-tuple-element.5) | data formatting | bytes 55296

commit v2 on v1

--- a/solution.py
+++ b/solution.py
@@ -11,6 +11,7 @@
 ITERS = 2
 REACH = 2
 SPAN = 2 * REACH + 1
+ORDER = sorted(range(-REACH, REACH + 1), key=abs)
 LANES = 128
 ROWS = 8
 MESH = pl.DeviceIdType.MESH
@@ -99,11 +100,11 @@
         return (lax.rem(cell + delta + cells, cells), lax.rem(grp + turn, grps))
 
     def slot_index(delta, turn):
-        return (delta % SPAN) * grps + turn % grps
+        return ORDER.index(delta) * grps + turn % grps
 
     def peers(reach):
         found = []
-        for delta in sorted(range(-reach, reach + 1), key=lambda d: -abs(d)):
+        for delta in sorted(range(-reach, reach + 1), key=abs):
             for turn in range(grps):
                 if delta != 0 or turn != 0:
                     found.append((delta, turn))
@@ -121,8 +122,8 @@
     own_rows = [row9 == 2 * b + (lane9 >= CAM_TILE).astype(jnp.int32) for b in range(chunks)]
 
     live = [s < load[0] for s in range(slots)]
-    ids = [pattern[s, 0] for s in range(slots)]
-    point_ids = [pattern[s, 1] for s in range(slots)]
+    ids = [pattern[0, s] for s in range(slots)]
+    point_ids = [pattern[1, s] for s in range(slots)]
     id_rows = jnp.full((ROWS, LANES), -4096, jnp.int32)
     point_rows = jnp.full((ROWS, LANES), -1, jnp.int32)
     for s in range(slots):
@@ -251,10 +252,10 @@
             energy_lanes = energy_lanes + energy[:, i * LANES : (i + 1) * LANES]
         return backward, jnp.sum(energy_lanes, axis=0, keepdims=True)
 
-    def send_slots(turn_no, backward):
+    def send_slots(turn_no, backward, reach):
         slot_send[turn_no] = backward
         slot_recv[turn_no, 0] = backward
-        for delta, turn in peers(REACH):
+        for delta, turn in peers(reach):
             pltpu.make_async_remote_copy(
                 src_ref=slot_send.at[turn_no],
                 dst_ref=slot_recv.at[turn_no, slot_index(-delta, -turn)],
@@ -265,14 +266,18 @@
             ).start()
 
     others = pl.ds(1, SPAN * grps - 1)
+    closer = pl.ds(1, 3 * grps - 1)
 
     def wait_bytes(ref, sem):
         pltpu.make_async_copy(ref, ref, sem).wait()
 
-    def gather_back(turn_no, chooser, sides):
-        wait_bytes(slot_recv.at[turn_no, others], slot_recv_sem.at[turn_no])
-        stacked = slot_recv[turn_no].astype(F32).reshape(SPAN * grps * ROWS, chunks * LANES)
-        summed = jnp.dot(chooser, stacked.astype(BF16), preferred_element_type=F32)
+    def gather_back(turn_no, chooser, sides, count):
+        wait_bytes(slot_recv.at[turn_no, pl.ds(1, count - 1)], slot_recv_sem.at[turn_no])
+        height = count * ROWS
+        stacked = slot_recv[turn_no, :count].astype(F32).reshape(height, chunks * LANES)
+        summed = jnp.dot(
+            chooser[:, :height], stacked.astype(BF16), preferred_element_type=F32
+        )
         fields = []
         for side in sides:
             parts = []
@@ -300,12 +305,11 @@
     for copy in jac_copies:
         copy.wait()
     backward, _ = slot_rows()
-    send_slots(0, backward)
+    send_slots(0, backward, REACH)
 
     wait_bytes(pattern_recv.at[others], pattern_sem.at[1])
     columns = []
-    for shift in range(SPAN):
-        delta = shift if shift <= REACH else shift - SPAN
+    for shift, delta in enumerate(ORDER):
         for turn in range(grps):
             at = pattern_recv[shift * grps + turn] + delta * tiles
             columns.append((at == lane8).astype(F32))
@@ -317,7 +321,7 @@
     for copy in halo_copies[2:]:
         copy.wait()
 
-    left, own, right_side = gather_back(0, chooser, (0, 1, 2))
+    left, own, right_side = gather_back(0, chooser, (0, 1, 2), SPAN * grps)
     residual0 = residual0 + jnp.concatenate(own, axis=1)
     direction = residual0 * scale
     put(1, blocks_of(direction))
@@ -346,10 +350,10 @@
         copy.start()
         image_copies.append(copy)
     backward, _ = slot_rows()
-    send_slots(1, backward)
+    send_slots(1, backward, REACH)
     for copy in image_copies:
         copy.wait()
-    left, own, right_side = gather_back(1, chooser, (0, 1, 2))
+    left, own, right_side = gather_back(1, chooser, (0, 1, 2), SPAN * grps)
     image1 = product1 - jnp.concatenate(own, axis=1)
     trial = residual0 - image1
     shaped = trial * scale
@@ -365,7 +369,7 @@
             ],
         )
     backward, energy = slot_rows()
-    send_slots(2, backward)
+    send_slots(2, backward, 1)
     product2 = block_product(shaped)
 
     def lane_sum(field):
@@ -401,7 +405,7 @@
         return carry
 
     lax.fori_loop(1, devices, spread_scalars, 0)
-    (own,) = gather_back(2, chooser, (1,))
+    (own,) = gather_back(2, chooser, (1,), 3 * grps)
     image2 = product2 - jnp.concatenate(own, axis=1)
     wait_bytes(scalar_recv, scalar_sem.at[1])
     totals = jnp.sum(sums + jnp.sum(scalar_recv[...], axis=0), axis=1, keepdims=True)
@@ -419,8 +423,21 @@
 
     wait_bytes(scalar_recv, scalar_sem.at[0])
     wait_bytes(pattern_recv.at[others], pattern_sem.at[0])
-    for turn_no in range(3):
-        wait_bytes(slot_recv.at[turn_no, others], slot_send_sem.at[turn_no])
+    for turn_no, sent in enumerate((others, others, closer)):
+        wait_bytes(slot_recv.at[turn_no, sent], slot_send_sem.at[turn_no])
+
+
+def finish_kernel(first, second, solution_ref, residual_ref):
+    solution_ref[...] = first[...]
+    residual_ref[...] = second[...]
+
+
+def finish(first, second):
+    vmem = pl.BlockSpec(memory_space=pltpu.VMEM)
+    shape = jax.ShapeDtypeStruct(first.shape, first.dtype)
+    return pl.pallas_call(
+        finish_kernel, out_shape=(shape, shape), in_specs=[vmem] * 2, out_specs=(vmem, vmem)
+    )(first, second)
 
 
 def per_device(
@@ -436,7 +453,7 @@
     vmem = pl.BlockSpec(memory_space=pltpu.VMEM)
     dma = pltpu.SemaphoreType.DMA
     field = jax.ShapeDtypeStruct((params, cameras), F32)
-    return pl.pallas_call(
+    first, second = pl.pallas_call(
         functools.partial(kernel, cells, grps),
         out_shape=(field, field),
         in_specs=[hbm] * 5 + [smem] * 2,
@@ -472,7 +489,8 @@
             dma((2,)),
         ],
         compiler_params=pltpu.CompilerParams(collective_id=0, has_side_effects=True),
-    )(initial_guess, right_side, camera_blocks, point_inverse, jacobian_tiles, tile_pattern, cell_load)
+    )(initial_guess, right_side, camera_blocks, point_inverse, jacobian_tiles, tile_pattern.T, cell_load)
+    return finish(first, second)
 
 
 def solution(mesh):

time: 41.9 us -> 36 us (0.86)
  local copies, waits for them, and re-layouts: 4.19 us -> 0 us
  Pallas kernels: 36.1 us -> 34.5 us
    unnamed x3 -> x0, local copies, waits for them, and re-layouts: 4.19 us -> none
    pallas_call x1, Pallas kernels: 36.1 us -> 33 us  [per_device(): pl.pallas_call(functools.partial(kernel, cells, grps), out_shape=(field,...]
    pallas_call x0 -> x1, Pallas kernels: none -> 1.46 us  [finish(): pl.pallas_call(finish_kernel, out_shape=(shape, shape), in_specs=[vmem] *...]
where the time goes in v2:
time: 36 us; the launch traced here: 35.8 us
  Pallas kernels  34.5 us (96%)
  between operations  1.29 us (4%)
    pallas_call x1, Pallas kernels, per_device(): pl.pallas_call(functools.partial(kernel, cells, grps), out_shape=(field,...  33 us
    pallas_call x1, Pallas kernels, finish(): pl.pallas_call(finish_kernel, out_shape=(shape, shape), in_specs=[vmem] *...  1.46 us

profile of v2, /device:TPU:0, one launch (start us, length us, event | category | flops | bytes accessed | tf_op | source)
XLA Modules:
  0.0 35.8 jit_solution(170596639159991898)
XLA Ops:
  1.3 33.0 %shard_map.86 = (f32[9,768]{1,0:T(8,128)}, f32[9,768]{1,0:T(8,128)}) custom-call(f32[9,768]{1,0:T(8,128)} %guess_hbm.1, f32[9,768]{1,0:T(8,128)} %right_hbm.1, f32[9,9,768]{2,1,0:T(8,128)} %blocks_hbm.1, f32[3,3,512]{2,1,0:T(4,128)} %inverse_hbm.1, bf16[6,576,384]{2,1,0:T(8,128)(2,1)} %jac_hbm.1, s32[2,6]{1,0:T(2,128)} %bitcast.1, s32[1]{0:T(128)S(6)} %copy.9.load), custom_call_target="tpu_custom_call" | custom-call | tf_op jit(solution)/shard_map/pallas_call | solution.py:456
  34.3 1.5 %shard_map.87 = (f32[9,768]{1,0:T(8,128)}, f32[9,768]{1,0:T(8,128)}) custom-call(f32[9,768]{1,0:T(8,128)} %get-tuple-element.4.first, f32[9,768]{1,0:T(8,128)} %get-tuple-element.5.second), custom_call_target="tpu_custom_call" | custom-call | tf_op jit(solution)/shard_map/pallas_call | solution.py:438

commit v3 on v2

--- a/solution.py
+++ b/solution.py
@@ -69,7 +69,6 @@
     devices = cells * grps
     cell = lax.axis_index("cell")
     grp = lax.axis_index("grp")
-    me = cell * grps + grp
 
     local = [
         pltpu.make_async_copy(src, dst, local_sem.at[i])
@@ -87,14 +86,24 @@
 
     barrier = pltpu.get_barrier_semaphore()
 
-    def greet(i, carry):
-        other = lax.rem(me + i, devices)
-        pl.semaphore_signal(
-            barrier, inc=1, device_id=(other // grps, lax.rem(other, grps)), device_id_type=MESH
-        )
-        return carry
-
-    lax.fori_loop(1, devices, greet, 0)
+    turned = [lax.rem(grp + turn, grps) for turn in range(grps)]
+
+    def everyone(act):
+        for turn in range(1, grps):
+            act(turn - 1, (cell, turned[turn]))
+
+        def one_cell(delta, carry):
+            other = lax.rem(cell + delta, cells)
+            for turn in range(grps):
+                act(delta * grps + (turn - 1), (other, turned[turn]))
+            return carry
+
+        lax.fori_loop(1, cells, one_cell, 0)
+
+    def greet(index, device):
+        pl.semaphore_signal(barrier, inc=1, device_id=device, device_id_type=MESH)
+
+    everyone(greet)
 
     def near(delta, turn):
         return (lax.rem(cell + delta + cells, cells), lax.rem(grp + turn, grps))
@@ -108,7 +117,7 @@
             for turn in range(grps):
                 if delta != 0 or turn != 0:
                     found.append((delta, turn))
-        return found
+        return sorted(found, key=lambda peer: (abs(peer[0]), -peer[1]))
 
     def iota(shape, axis):
         return lax.broadcasted_iota(jnp.int32, shape, axis)
@@ -392,19 +401,17 @@
         sums = jnp.where(row8 == i, value, sums)
     scalar_send[...] = sums
 
-    def spread_scalars(i, carry):
-        other = lax.rem(me + i, devices)
+    def send_scalars(index, device):
         pltpu.make_async_remote_copy(
             src_ref=scalar_send,
-            dst_ref=scalar_recv.at[i - 1],
+            dst_ref=scalar_recv.at[index],
             send_sem=scalar_sem.at[0],
             recv_sem=scalar_sem.at[1],
-            device_id=(other // grps, lax.rem(other, grps)),
+            device_id=device,
             device_id_type=MESH,
         ).start()
-        return carry
-
-    lax.fori_loop(1, devices, spread_scalars, 0)
+
+    everyone(send_scalars)
     (own,) = gather_back(2, chooser, (1,), 3 * grps)
     image2 = product2 - jnp.concatenate(own, axis=1)
     wait_bytes(scalar_recv, scalar_sem.at[1])

time: 36 us -> 35.8 us (level)
  no operation moved by 1% of the time
where the time goes in v3:
time: 35.8 us; the launch traced here: 35.6 us
  Pallas kernels  34.3 us (96%)
  between operations  1.29 us (4%)
    pallas_call x1, Pallas kernels, per_device(): pl.pallas_call(functools.partial(kernel, cells, grps), out_shape=(field,...  32.8 us
    pallas_call x1, Pallas kernels, finish(): pl.pallas_call(finish_kernel, out_shape=(shape, shape), in_specs=[vmem] *...  1.46 us

profile of v3, /device:TPU:0, one launch (start us, length us, event | category | flops | bytes accessed | tf_op | source)
XLA Modules:
  0.0 35.6 jit_solution(7557824908289096616)
XLA Ops:
  1.3 32.8 %shard_map.86 = (f32[9,768]{1,0:T(8,128)}, f32[9,768]{1,0:T(8,128)}) custom-call(f32[9,768]{1,0:T(8,128)} %guess_hbm.1, f32[9,768]{1,0:T(8,128)} %right_hbm.1, f32[9,9,768]{2,1,0:T(8,128)} %blocks_hbm.1, f32[3,3,512]{2,1,0:T(4,128)} %inverse_hbm.1, bf16[6,576,384]{2,1,0:T(8,128)(2,1)} %jac_hbm.1, s32[2,6]{1,0:T(2,128)} %bitcast.1, s32[1]{0:T(128)S(6)} %copy.9.load), custom_call_target="tpu_custom_call" | custom-call | tf_op jit(solution)/shard_map/pallas_call | solution.py:463
  34.1 1.5 %shard_map.87 = (f32[9,768]{1,0:T(8,128)}, f32[9,768]{1,0:T(8,128)}) custom-call(f32[9,768]{1,0:T(8,128)} %get-tuple-element.4.first, f32[9,768]{1,0:T(8,128)} %get-tuple-element.5.second), custom_call_target="tpu_custom_call" | custom-call | tf_op jit(solution)/shard_map/pallas_call | solution.py:445
